TPU v7x, 128 devices: a whole 4x4x4 slice. The times are simulated.
128 devices in a mesh: dp: 16 (over x, z_lo, core), tensor: 8 (over z_hi, y).
Axes of the slice: x: 4, y: 4, z: 4 (z_hi: 2, z_lo: 2; z = z_hi * 2 + z_lo), core: 2. Of those that a mesh axis runs over, the one named last changes fastest.
Arguments:
- tokens: bfloat16 [8192, 2048], P('dp'), may hold values from -6 to 6
- first_gain: float32 [2048], replicated, may hold values from 0.5 to 1.5
- first_shift: float32 [2048], replicated, may hold values from -1.75 to 1.75
- query_weight: float32 [2048, 2048], P('dp', 'tensor'), may hold values from -0.125 to 0.125
- query_bias: float32 [2048], P('tensor'), may hold values from -3 to 3
- key_weight: float32 [2048, 2048], P('dp', 'tensor'), may hold values from -0.125 to 0.125
- value_weight: float32 [2048, 2048], P('dp', 'tensor'), may hold values from -0.125 to 0.125
- value_bias: float32 [2048], P('tensor'), may hold values from -3 to 3
- out_weight: float32 [2048, 2048], P('tensor', 'dp'), may hold values from -0.5 to 0.5
- out_bias: float32 [2048], replicated, may hold values from -1.75 to 1.75
- second_gain: float32 [2048], replicated, may hold values from 0.5 to 1.5
- second_shift: float32 [2048], replicated, may hold values from -1.75 to 1.75
- up_weight: float32 [2048, 8192], P('dp', 'tensor'), may hold values from -0.125 to 0.125
- up_bias: float32 [8192], P('tensor'), may hold values from -3 to 3
- down_weight: float32 [8192, 2048], P('tensor', 'dp'), may hold values from -0.0625 to 0.0625
- down_bias: float32 [2048], replicated, may hold values from -1.75 to 1.75
- cotangent: bfloat16 [8192, 2048], P('dp'), may hold values from -6 to 6
- prefix: int32 [1], replicated, may hold values from 819 to 4096
- block_order: int32 [32], replicated, may hold values from 0 to 31, as said below
Outputs:
- layer_out: bfloat16 [8192, 2048], P('dp')
- tokens_grad: float32 [8192, 2048], P('dp')
- first_gain_grad: float32 [2048], replicated
- first_shift_grad: float32 [2048], replicated
- query_weight_grad: float32 [2048, 2048], P('dp', 'tensor')
- query_bias_grad: float32 [2048], P('tensor')
- key_weight_grad: float32 [2048, 2048], P('dp', 'tensor')
- value_weight_grad: float32 [2048, 2048], P('dp', 'tensor')
- value_bias_grad: float32 [2048], P('tensor')
- out_weight_grad: float32 [2048, 2048], P('tensor', 'dp')
- out_bias_grad: float32 [2048], replicated
- second_gain_grad: float32 [2048], replicated
- second_shift_grad: float32 [2048], replicated
- up_weight_grad: float32 [2048, 8192], P('dp', 'tensor')
- up_bias_grad: float32 [8192], P('tensor')
- down_weight_grad: float32 [8192, 2048], P('tensor', 'dp')
- down_bias_grad: float32 [2048], replicated
Inputs may be any that keep to these rules, and one draw needn't show every extreme that they name: `block_order`: for each sequence s, entries s * 32 to s * 32 + 31 are a permutation of those same numbers: every stored block lies in its own sequence's rows, but its place within the sequence is shuffled.
All inputs are finite; a program needn't handle non-finite values.
Results may differ from a plain program's by a relative error of at most 0.025.
Values may be sent and summed in bfloat16 or wider, within the bound.
A program may use at most 192 MiB of HBM per device.

v0:
```python
import math
import jax
import jax.numpy as jnp
from jax import lax
from jax.sharding import PartitionSpec as P

HEAD = 128
epsilon = 1e-05
masked_score = -1e30


def sent_together(arrays, axis, dim, along):
    both = jnp.concatenate(arrays, axis=along)
    filled, at, gathered = (lax.all_gather(both, axis, axis=dim, tiled=True), 0, [])
    for a in arrays:
        gathered.append(lax.slice_in_dim(filled, at, at + a.shape[along], axis=along))
        at += a.shape[along]
    return tuple(gathered)


def in_one_piece(arrays, axis, dim, along):
    ends, at = ([], 0)
    for a in arrays[:-1]:
        at += a.shape[along]
        ends.append(at)
    both = jnp.concatenate(arrays, axis=along)
    return tuple(
        jnp.split(lax.psum_scatter(both, axis, scatter_dimension=dim, tiled=True), ends, axis=along)
    )


def from_everyone(value, axis):
    copies = jnp.broadcast_to(value, (lax.axis_size(axis), *value.shape))
    return lax.all_to_all(copies, axis, split_axis=0, concat_axis=0, tiled=True)


def over_copies(value, axis):
    return from_everyone(value, axis).astype(jnp.float32).sum(axis=0)


def to_low(values_in):
    return values_in.astype(jnp.bfloat16)


def matmul(left_side, right_side):
    return jnp.dot(left_side, right_side, preferred_element_type=jnp.float32)


def rows_inner(left_side, right_side):
    return lax.dot_general(
        left_side, right_side, (((0,), (0,)), ((), ())), preferred_element_type=jnp.float32
    )


def cols_inner(left_side, right_side):
    return lax.dot_general(
        left_side, right_side, (((1,), (1,)), ((), ())), preferred_element_type=jnp.float32
    )


def norm_forward(values_in, norm_gain, norm_shift):
    average = jnp.mean(values_in, axis=-1, keepdims=True)
    centred = values_in - average
    variance = jnp.mean(centred * centred, axis=-1, keepdims=True)
    inverse = lax.rsqrt(variance + epsilon)
    scaled = centred * inverse
    return (scaled * norm_gain + norm_shift, scaled, inverse)


def norm_backward(grad_out, scaled, inverse, norm_gain):
    grad_scaled = grad_out * norm_gain
    first_mean = jnp.mean(grad_scaled, axis=-1, keepdims=True)
    second = jnp.mean(grad_scaled * scaled, axis=-1, keepdims=True)
    return inverse * (grad_scaled - first_mean - scaled * second)


def place_of(row_ids, block_order, block_rows, blocks_per_seq):
    blocks = row_ids // block_rows
    table_size = block_order.shape[0]
    matches = blocks[:, None] == jnp.arange(table_size, dtype=jnp.int32)[None, :]
    orders = jnp.sum(jnp.where(matches, block_order[None, :], 0), axis=1)
    return (orders % blocks_per_seq * block_rows + row_ids % block_rows, blocks // blocks_per_seq)


def on_device(
    tokens,
    first_gain,
    first_shift,
    query_weight,
    query_bias,
    key_weight,
    value_weight,
    value_bias,
    out_weight,
    out_bias,
    second_gain,
    second_shift,
    up_weight,
    up_bias,
    down_weight,
    down_bias,
    cotangent,
    prefix,
    block_order,
):
    row_count = tokens.shape[0]
    head_total = query_weight.shape[1] // HEAD
    head_width = head_total * HEAD
    seq_len = row_count * lax.axis_size("dp")
    block_rows = row_count // 2
    blocks_per_seq = seq_len // block_rows
    score_scale = 1.0 / math.sqrt(HEAD)
    dp_index = lax.axis_index("dp")
    own_rows = dp_index * row_count + jnp.arange(row_count, dtype=jnp.int32)
    query_places, query_seqs = place_of(own_rows, block_order, block_rows, blocks_per_seq)
    seq_count = prefix.shape[0]
    seq_match = query_seqs[:, None] == jnp.arange(seq_count, dtype=jnp.int32)[None, :]
    query_limits = jnp.sum(jnp.where(seq_match, prefix[None, :], 0), axis=1)

    def key_mask(first_row, key_width):
        key_rows = first_row + jnp.arange(key_width, dtype=jnp.int32)
        key_places, key_seqs = place_of(key_rows, block_order, block_rows, blocks_per_seq)
        same_seq = key_seqs[None, :] == query_seqs[:, None]
        before = (key_places[None, :] <= query_places[:, None]) | (
            key_places[None, :] < query_limits[:, None]
        )
        return same_seq & before

    rows_gathered = sent_together(
        (to_low(query_weight), to_low(key_weight), to_low(value_weight), to_low(up_weight)),
        "dp",
        0,
        1,
    )
    query_all, key_all, value_all, up_all = rows_gathered
    cols_gathered = sent_together((to_low(out_weight), to_low(down_weight)), "dp", 1, 0)
    out_all, down_all = cols_gathered
    residual = tokens.astype(jnp.float32)
    normed, scaled_one, inverse_one = norm_forward(residual, first_gain, first_shift)
    normed_low = to_low(normed)
    queries = to_low(matmul(normed_low, query_all) + query_bias)
    keys_local = to_low(matmul(normed_low, key_all))
    values_local = to_low(matmul(normed_low, value_all) + value_bias)
    query_heads = queries.reshape(row_count, head_total, HEAD)

    def split_blocks(key_part, value_part):
        part_rows = key_part.shape[0]
        block_width = math.gcd(part_rows, 512)
        block_count = part_rows // block_width
        key_blocks = key_part.reshape(block_count, block_width, head_total, HEAD)
        value_blocks = value_part.reshape(block_count, block_width, head_total, HEAD)
        return (block_width, (key_blocks, value_blocks, jnp.arange(block_count, dtype=jnp.int32)))

    def block_scores(key_block):
        return (
            jnp.einsum("qhd,khd->hqk", query_heads, key_block, preferred_element_type=jnp.float32)
            * score_scale
        )

    key_source, value_source = sent_together((keys_local, values_local), "dp", 0, 1)
    source_start = 0
    block_width, block_items = split_blocks(key_source, value_source)

    def advance(state_now, block_item):
        key_block, value_block, block_index = block_item
        allowed = key_mask(source_start + block_index * block_width, block_width)

        def compute(state_old):
            row_max, row_sum = state_old
            scores = jnp.where(allowed[None], block_scores(key_block), masked_score)
            new_max = jnp.maximum(row_max, jnp.max(scores, axis=-1))
            exponent = jnp.where(allowed[None], jnp.exp(scores - new_max[..., None]), 0.0)
            return (new_max, row_sum * jnp.exp(row_max - new_max) + jnp.sum(exponent, axis=-1))

        return (lax.cond(jnp.any(allowed), compute, lambda state_old: state_old, state_now), None)

    initial = (
        jnp.full((head_total, row_count), masked_score, jnp.float32),
        jnp.zeros((head_total, row_count), jnp.float32),
    )
    running, _ = lax.scan(advance, initial, block_items)
    row_max, row_sum = running
    log_total = row_max + jnp.log(row_sum)
    attention_block_width, block_items = split_blocks(key_source, value_source)

    def advance(weighted, block_item):
        key_block, value_block, block_index = block_item
        allowed = key_mask(
            source_start + block_index * attention_block_width, attention_block_width
        )

        def compute(weighted_old):
            probs = jnp.where(
                allowed[None], jnp.exp(block_scores(key_block) - log_total[..., None]), 0.0
            )
            return weighted_old + jnp.einsum(
                "hqk,khd->hqd", to_low(probs), value_block, preferred_element_type=jnp.float32
            )

        return (
            lax.cond(jnp.any(allowed), compute, lambda weighted_old: weighted_old, weighted),
            None,
        )

    start = jnp.zeros((head_total, row_count, HEAD), jnp.float32)
    weighted, _ = lax.scan(advance, start, block_items)
    mixed_low = to_low(weighted.transpose(1, 0, 2).reshape(row_count, head_width))
    branch = (
        lax.psum(matmul(mixed_low, out_all).astype(jnp.bfloat16), "tensor").astype(jnp.float32)
        + out_bias
    )
    middle = residual + branch
    normed_two, scaled_two, inverse_two = norm_forward(middle, second_gain, second_shift)
    normed_two_low = to_low(normed_two)
    pre_act = matmul(normed_two_low, up_all) + up_bias
    hidden, gelu_back = jax.vjp(lambda inputs: jax.nn.gelu(inputs, approximate=False), pre_act)
    hidden_low = to_low(hidden)
    out_branch = (
        lax.psum(matmul(hidden_low, down_all).astype(jnp.bfloat16), "tensor").astype(jnp.float32)
        + down_bias
    )
    output = middle + out_branch
    grad_out = cotangent.astype(jnp.float32)
    grad_down_bias = jnp.sum(grad_out, axis=0)
    grad_down = rows_inner(hidden_low, cotangent)
    grad_hidden = cols_inner(cotangent, down_all)
    grad_pre_low = to_low(gelu_back(grad_hidden)[0])
    grad_up_bias = jnp.sum(grad_pre_low.astype(jnp.float32), axis=0)
    grad_up = rows_inner(normed_two_low, grad_pre_low)
    grad_normed_two = lax.psum(
        cols_inner(grad_pre_low, up_all).astype(jnp.bfloat16), "tensor"
    ).astype(jnp.float32)
    grad_gain_two = jnp.sum(grad_normed_two * scaled_two, axis=0)
    grad_shift_two = jnp.sum(grad_normed_two, axis=0)
    grad_middle = grad_out + norm_backward(grad_normed_two, scaled_two, inverse_two, second_gain)
    grad_middle_low = to_low(grad_middle)
    grad_out_bias = jnp.sum(grad_middle_low.astype(jnp.float32), axis=0)
    grad_out_weight = rows_inner(mixed_low, grad_middle_low)
    grad_mixed_low = to_low(cols_inner(grad_middle_low, out_all))
    grad_heads = grad_mixed_low.reshape(row_count, head_total, HEAD)
    row_delta = jnp.sum(grad_heads.astype(jnp.float32).transpose(1, 0, 2) * weighted, axis=-1)
    part_rows = key_source.shape[0]
    attend_block_width, block_items = split_blocks(key_source, value_source)

    def advance(grad_query, block_item):
        key_block, value_block, block_index = block_item
        allowed = key_mask(source_start + block_index * attend_block_width, attend_block_width)

        def compute(grad_now):
            probs = jnp.where(
                allowed[None], jnp.exp(block_scores(key_block) - log_total[..., None]), 0.0
            )
            grad_probs = jnp.einsum(
                "qhd,khd->hqk", grad_heads, value_block, preferred_element_type=jnp.float32
            )
            grad_scores = to_low(probs * (grad_probs - row_delta[..., None]))
            new_grad = (
                grad_now
                + jnp.einsum(
                    "hqk,khd->qhd", grad_scores, key_block, preferred_element_type=jnp.float32
                )
                * score_scale
            )
            grad_key = (
                jnp.einsum(
                    "hqk,qhd->khd", grad_scores, query_heads, preferred_element_type=jnp.float32
                )
                * score_scale
            )
            grad_value = jnp.einsum(
                "hqk,qhd->khd", to_low(probs), grad_heads, preferred_element_type=jnp.float32
            )
            return (new_grad, grad_key, grad_value)

        def skipped(grad_now):
            zero_block = jnp.zeros((attend_block_width, head_total, HEAD), jnp.float32)
            return (grad_now, zero_block, zero_block)

        new_grad, grad_key, grad_value = lax.cond(jnp.any(allowed), compute, skipped, grad_query)
        return (new_grad, (grad_key, grad_value))

    start_grad = jnp.zeros((row_count, head_total, HEAD), jnp.float32)
    grad_query, key_terms = lax.scan(advance, start_grad, block_items)
    grad_query, key_term, value_term = (
        grad_query,
        key_terms[0].reshape(part_rows, head_width),
        key_terms[1].reshape(part_rows, head_width),
    )
    grad_keys, grad_values = tuple(
        (
            part.astype(jnp.float32)
            for part in in_one_piece(
                (key_term.astype(jnp.bfloat16), value_term.astype(jnp.bfloat16)), "dp", 0, 1
            )
        )
    )
    grad_query_low = to_low(grad_query.reshape(row_count, head_width))
    grad_keys_low = to_low(grad_keys)
    grad_values_low = to_low(grad_values)
    grad_query_bias = jnp.sum(grad_query_low.astype(jnp.float32), axis=0)
    grad_value_bias = jnp.sum(grad_values_low.astype(jnp.float32), axis=0)
    grad_query_weight = rows_inner(normed_low, grad_query_low)
    grad_key_weight = rows_inner(normed_low, grad_keys_low)
    grad_value_weight = rows_inner(normed_low, grad_values_low)
    local_normed = (
        cols_inner(grad_query_low, query_all)
        + cols_inner(grad_keys_low, key_all)
        + cols_inner(grad_values_low, value_all)
    )
    grad_normed_one = lax.psum(local_normed.astype(jnp.bfloat16), "tensor").astype(jnp.float32)
    grad_gain_one = jnp.sum(grad_normed_one * scaled_one, axis=0)
    grad_shift_one = jnp.sum(grad_normed_one, axis=0)
    grad_tokens = grad_middle + norm_backward(grad_normed_one, scaled_one, inverse_one, first_gain)
    row_sums = tuple(
        (
            part.astype(jnp.float32)
            for part in in_one_piece(
                (
                    grad_query_weight.astype(jnp.bfloat16),
                    grad_key_weight.astype(jnp.bfloat16),
                    grad_value_weight.astype(jnp.bfloat16),
                    grad_up.astype(jnp.bfloat16),
                ),
                "dp",
                0,
                1,
            )
        )
    )
    column_sums = tuple(
        (
            part.astype(jnp.float32)
            for part in in_one_piece(
                (grad_out_weight.astype(jnp.bfloat16), grad_down.astype(jnp.bfloat16)), "dp", 1, 0
            )
        )
    )
    small_sums = (
        over_copies(grad_gain_one.astype(jnp.bfloat16), "dp").astype(jnp.float32),
        over_copies(grad_shift_one.astype(jnp.bfloat16), "dp").astype(jnp.float32),
        over_copies(grad_query_bias.astype(jnp.bfloat16), "dp").astype(jnp.float32),
        over_copies(grad_value_bias.astype(jnp.bfloat16), "dp").astype(jnp.float32),
        over_copies(grad_out_bias.astype(jnp.bfloat16), "dp").astype(jnp.float32),
        over_copies(grad_gain_two.astype(jnp.bfloat16), "dp").astype(jnp.float32),
        over_copies(grad_shift_two.astype(jnp.bfloat16), "dp").astype(jnp.float32),
        over_copies(grad_up_bias.astype(jnp.bfloat16), "dp").astype(jnp.float32),
        over_copies(grad_down_bias.astype(jnp.bfloat16), "dp").astype(jnp.float32),
    )
    return (
        output.astype(jnp.bfloat16),
        grad_tokens,
        small_sums[0],
        small_sums[1],
        row_sums[0],
        small_sums[2],
        row_sums[1],
        row_sums[2],
        small_sums[3],
        column_sums[0],
        small_sums[4],
        small_sums[5],
        small_sums[6],
        row_sums[3],
        small_sums[7],
        column_sums[1],
        small_sums[8],
    )


def solution(mesh):
    return jax.shard_map(
        on_device,
        mesh=mesh,
        in_specs=(
            P("dp", None),
            P(),
            P(),
            P("dp", "tensor"),
            P("tensor"),
            P("dp", "tensor"),
            P("dp", "tensor"),
            P("tensor"),
            P("tensor", "dp"),
            P(),
            P(),
            P(),
            P("dp", "tensor"),
            P("tensor"),
            P("tensor", "dp"),
            P(),
            P("dp", None),
            P(),
            P(),
        ),
        out_specs=(
            P("dp", None),
            P("dp", None),
            P(),
            P(),
            P("dp", "tensor"),
            P("tensor"),
            P("dp", "tensor"),
            P("dp", "tensor"),
            P("tensor"),
            P("tensor", "dp"),
            P(),
            P(),
            P(),
            P("dp", "tensor"),
            P("tensor"),
            P("tensor", "dp"),
            P(),
        ),
        check_vma=False,
    )
```

profile of v0, /device:TPU:3, one launch (start us, length us, event | category | flops | bytes accessed | tf_op | source)
XLA Modules:
  0.0 1173.7 jit_solution(17197489712279023680)
XLA Ops:
  15.4 46.7 %all-gather.4.cloned.1.call-done = bf16[2048,1792]{1,0:T(8,128)(2,1)} async-done(((bf16[128,1792]{1,0:T(8,128)(2,1)}), bf16[2048,1792]{1,0:T(8,128)(2,1)}) %all-gather.4.cloned.1.call-update) | async-done | bytes 7340048 | tf_op jit(solution)/shard_map/all_gather | solution.py:14
  72.3 49.0 %all-gather.6.cloned.1.call-done = bf16[8192,512]{0,1:T(8,128)(2,1)} async-done(((bf16[512,512]{0,1:T(8,128)(2,1)}), bf16[8192,512]{0,1:T(8,128)(2,1)}) %all-gather.6.cloned.1.call-update) | async-done | bytes 8388624 | tf_op jit(solution)/shard_map/all_gather | solution.py:14
  130.2 7.9 copy.143
  138.1 76.3 %while.57 = (s32[]{:T(128)}, f32[2,512]{1,0:T(2,128)S(1)}, f32[2,512]{1,0:T(2,128)S(1)}, s32[16]{0:T(128)S(1)}, s32[32]{0:T(128)S(1)}, /*index=5*/s32[512]{0:T(5...) while((s32[]{:T(128)}, f32[2,512]{1,0:T(2,128)S(1)}, ...), condition=%wide.region_10.11_spmd.clone.clone, body=%wide.region_3.0_spmd.clone.clone.sunk | while | flops 140081152 | bytes 5585795 | solution.py:181
  214.4 6.0 copy.181
  220.4 7.9 copy.145
  228.3 76.4 %while.58 = (s32[]{:T(128)}, f32[2,512,128]{2,1,0:T(8,128)S(1)}, s32[16]{0:T(128)S(1)}, s32[32]{0:T(128)S(1)}, s32[512]{0:T(512)S(1)}, /*index=5*/bf16[16,512,2,...) while((s32[]{:T(128)}, f32[2,512,128]{2,1,0:T(8,128)S(1)}, ...), condition=%wide.region_16.17_spmd.clone.clone, body=%wide.region_11.16_spmd.clone.clone.sunk | while | flops 272330752 | bytes 2391411 | solution.py:206
  309.0 122.2 %all-reduce.5.cloned.1.call-done = bf16[512,2048]{1,0:T(8,128)(2,1)} async-done(((bf16[512,2048]{1,0:T(8,128)(2,1)}), bf16[512,2048]{1,0:T(8,128)(2,1)}) %all-reduce.5.cloned.1.call-update) | async-done | bytes 2097168 | tf_op jit(solution)/shard_map/psum | solution.py:209
  434.8 10.5 multiply_convert_fusion
  453.3 91.3 %all-reduce.7.cloned.1.call-done = bf16[512,2048]{1,0:T(8,128)(2,1)} async-done(((bf16[512,2048]{1,0:T(8,128)(2,1)}), bf16[512,2048]{1,0:T(8,128)(2,1)}) %all-reduce.7.cloned.1.call-update) | async-done | bytes 2097168 | tf_op jit(solution)/shard_map/psum | solution.py:230
  557.1 140.2 %while.59 = (s32[]{:T(128)}, f32[512,2,128]{2,0,1:T(8,128)S(1)}, bf16[16,512,2,128]{3,1,2,0:T(8,128)(2,1)}, bf16[16,512,2,128]{3,1,2,0:T(8,128)(2,1)}, s32[16]{0...) while((s32[]{:T(128)}, f32[512,2,128]{2,0,1:T(8,128)S(1)}, ...), condition=%wide.region_30.31_spmd.clone.clone, body=%wide.region_25.30_spmd.clone.clone.sunk | while | flops 676950016 | bytes 15504335 | solution.py:283
  697.3 7.8 copy.154
  705.2 8.5 copy.183
  713.6 8.0 copy.153
  721.6 8.5 copy.182
  730.1 7.7 pad_maximum_fusion
  745.9 7.9 copy.172
  754.3 6.2 fusion.121
  764.6 118.1 %reduce-scatter.8.cloned.1.call-done = bf16[512,512]{0,1:T(8,128)(2,1)} async-done(((bf16[8192,512]{0,1:T(8,128)(2,1)}), bf16[512,512]{0,1:T(8,128)(2,1)}) %reduce-scatter.8.cloned.1.call-update) | async-done | bytes 524304 | tf_op jit(solution)/shard_map/reduce_scatter | solution.py:28
  899.5 10.1 copy.170
  911.7 6.3 all-to-all-start.7
  985.0 86.7 %all-reduce.9.cloned.1.call-done = (bf16[512,2048]{1,0:T(8,128)(2,1)}, bf16[512,2048]{1,0:T(8,128)(2,1)}) async-done(((bf16[512,2048]{1,0:T(8,128)(2,1)}, bf16[512,2048]{1,0:T(8,128)(2,1)}), (bf16[512,2048]{1,0:T(8,128)(2,1)}, bf16[512,2048]{1,0:T(8,128)(2,1)})) %all-reduce.9.cloned.1.call-update) | async-done | bytes 4194320 | tf_op jit(solution)/shard_map/psum | solution.py:219
  1092.5 7.2 fusion.101
  1101.1 60.2 %reduce-scatter.10.cloned.1.call-done = bf16[128,1792]{1,0:T(8,128)(2,1)} async-done(((bf16[2048,1792]{1,0:T(8,128)(2,1)}), bf16[128,1792]{1,0:T(8,128)(2,1)}) %reduce-scatter.10.cloned.1.call-update) | async-done | bytes 458768
  (727 shorter events, 490.5 us)
Async XLA Ops:
  7.2 54.8 %all-gather.4.cloned.1.call-start = ((), (), s32[]{:S(2)}) async-start(), calls=%async_computation.12 | async-start | bytes 7798784 | tf_op jit(solution)/shard_map/all_gather | solution.py:14
  12.0 109.3 %all-gather.6.cloned.1.call-start = ((), (), s32[]{:S(2)}) async-start(), calls=%async_computation.13 | async-start | bytes 8912896 | tf_op jit(solution)/shard_map/all_gather | solution.py:14
  68.2 236.8 %all-gather.8.cloned.1.call-start = ((), (), s32[]{:S(2)}) async-start(), calls=%async_computation.14 | async-start | bytes 5570560 | tf_op jit(solution)/shard_map/all_gather | solution.py:14
  69.1 362.1 %all-reduce.5.cloned.1.call-start = ((), (), s32[]{:S(2)}) async-start(), calls=%async_computation.15 | async-start | bytes 4194304 | tf_op jit(solution)/shard_map/psum | solution.py:209
  304.8 128.9 %copy-start.7 = (bf16[512,2,128]{2,0,1:T(8,128)(2,1)}, bf16[512,2,128]{2,0,1:T(8,128)(2,1)S(1)}, u32[]{:S(2)}) copy-start(bf16[512,2,128]{2,0,1:T(8,128)(2,1)S(1)} %get-tuple-element.1875) | copy-start | bytes 786436
  304.9 128.7 %copy-start.11 = (bf16[2,512,128]{1,2,0:T(8,128)(2,1)}, bf16[2,512,128]{1,2,0:T(8,128)(2,1)S(1)}, u32[]{:S(2)}) copy-start(bf16[2,512,128]{1,2,0:T(8,128)(2,1)S(1)} %copy.146) | copy-start | bytes 786436
  308.4 126.4 %copy-start.25 = (f32[2048]{0:T(1024)S(1)}, f32[2048]{0:T(1024)}, u32[]{:S(2)}) copy-start(f32[2048]{0:T(1024)} %param.41) | copy-start | bytes 24580
  308.4 236.2 %all-reduce.7.cloned.1.call-start = ((), (), s32[]{:S(2)}) async-start(), calls=%async_computation.16 | async-start | bytes 4194304 | tf_op jit(solution)/shard_map/psum | solution.py:230
  453.3 429.4 %reduce-scatter.8.cloned.1.call-start = ((), (), s32[]{:S(2)}) async-start(), calls=%async_computation.17 | async-start | bytes 8912896 | tf_op jit(solution)/shard_map/reduce_scatter | solution.py:28
  737.8 242.5 %reduce-scatter.12.cloned.1.call-start = ((), (), s32[]{:S(2)}) async-start(), calls=%async_computation.19 | async-start | bytes 5570560
  753.9 317.8 %all-reduce.9.cloned.1.call-start = ((), (), s32[]{:S(2)}) async-start(), calls=%async_computation.20 | async-start | bytes 8388608 | tf_op jit(solution)/shard_map/psum | solution.py:219
  888.7 272.6 %reduce-scatter.10.cloned.1.call-start = ((), (), s32[]{:S(2)}) async-start(), calls=%async_computation.18 | async-start | bytes 7798784
  909.6 162.1 %copy-start.20 = (f32[2048]{0:T(1024)S(1)}, f32[2048]{0:T(1024)}, u32[]{:S(2)}) copy-start(f32[2048]{0:T(1024)} %param.32) | copy-start | bytes 24580
  909.6 162.1 %copy-start.22 = (f32[512]{0:T(512)S(1)}, f32[512]{0:T(512)}, u32[]{:S(2)}) copy-start(f32[512]{0:T(512)} %copy-done.21) | copy-start | bytes 6148
  909.6 162.1 %copy-start.24 = (f32[512]{0:T(512)S(1)}, f32[512]{0:T(512)}, u32[]{:S(2)}) copy-start(f32[512]{0:T(512)} %copy-done.23) | copy-start | bytes 6148
  911.7 11.0 all-to-all-start.7
  922.7 9.3 all-to-all-start.2
  932.0 9.8 all-to-all-start.4
  941.9 9.9 all-to-all-start.5
  951.8 10.0 all-to-all-start.6
  961.8 9.6 all-to-all-start.8
  974.9 9.6 all-to-all-start.3
  1076.9 10.0 all-to-all-start
  1086.9 12.9 %all-to-all-start.1 = ((bf16[16,2,1024]{2,1,0:T(2,128)(2,1)}), bf16[16,2,1024]{2,1,0:T(2,128)(2,1)S(1)}, u32[]{:S(2)}, u32[]{:S(2)}) async-start(bf16[16,2,1024]{2,1,0:T(2,128)(2,1)} %reshape.433), calls=%async_computation.2 | async-start | bytes 131072 | tf_op jit(solution)/shard_map/all_to_all | solution.py:34
  (38 other events, 910.7 us)
Sparse Core Ops, SparseCore 0:
  12.2 49.8 all-gather.3
  68.3 52.9 all-gather.5
  123.5 50.0 all-gather.7
  308.5 122.6 all-reduce.4
  453.4 91.2 all-reduce.6
  737.9 144.7 reduce-scatter.7
  885.1 69.3 reduce-scatter.11
  957.6 114.0 all-reduce.8
  1074.1 87.1 reduce-scatter.9
where the time goes:
time: 1180 us; the launch traced here: 1170 us
  waiting for transfers between devices  594 us (50%)
  other arithmetic  164 us (14%)
  local copies, waits for them, and re-layouts  153 us (13%)
  matrix products  133 us (11%)
  loops' own time  65.5 us (6%)
  starting transfers between devices  48.9 us (4%)
  between operations  15 us (1%)
    psum x1, waiting for transfers between devices, on_device(): lax.psum(matmul(mixed_low, out_all).astype(jnp.bfloat16), 'tensor')  122 us
    reduce_scatter x1, waiting for transfers between devices, in_one_piece(): lax.psum_scatter(both, axis, scatter_dimension=dim, tiled=True)  118 us
    all_gather x3, waiting for transfers between devices, sent_together(): lax.all_gather(both, axis, axis=dim, tiled=True)  95.7 us
    psum x1, waiting for transfers between devices, on_device(): lax.psum(cols_inner(grad_pre_low, up_all).astype(jnp.bfloat16), 'tensor')  91.3 us
    psum x1, waiting for transfers between devices, on_device(): lax.psum(matmul(hidden_low, down_all).astype(jnp.bfloat16), 'tensor')  86.7 us
    unnamed x111, local copies, waits for them, and re-layouts  74.7 us
    unnamed x11, waiting for transfers between devices  60.3 us
    reduce_or x48, other arithmetic, advance(): jnp.any(allowed)  58 us
  transfers between devices with their start and end apart: 18, of which 15 were waited for; matrix products, arithmetic and copies ran while one was open for 20% of the time, Pallas kernels for 0%

commit v1 on v0

--- a/solution.py
+++ b/solution.py
@@ -206,7 +206,9 @@
     weighted, _ = lax.scan(advance, start, block_items)
     mixed_low = to_low(weighted.transpose(1, 0, 2).reshape(row_count, head_width))
     branch = (
-        lax.psum(matmul(mixed_low, out_all).astype(jnp.bfloat16), "tensor").astype(jnp.float32)
+        jnp.sum(
+            lax.all_gather(matmul(mixed_low, out_all).astype(jnp.bfloat16), "tensor"), axis=0
+        ).astype(jnp.float32)
         + out_bias
     )
     middle = residual + branch

time: 1180 us -> 1290 us (1.093)
  waiting for transfers between devices: 594 us -> 689 us
    all_gather x0 -> x1, waiting for transfers between devices: none -> 220 us  [on_device(): lax.all_gather(matmul(mixed_low, out_all).astype(jnp.bfloat16), 'tensor')]
    psum x1 -> x0, waiting for transfers between devices: 122 us -> none  [on_device(): lax.psum(matmul(mixed_low, out_all).astype(jnp.bfloat16), 'tensor')]
  transfers between devices with their start and end apart: 18 -> 18, of which waited for: 15 -> 15; matrix products, arithmetic and copies ran while one was open for 20% -> 19% of each run, Pallas kernels for 0% -> 0%
where the time goes in v1:
time: 1290 us; the launch traced here: 1280 us
  waiting for transfers between devices  689 us (53%)
  other arithmetic  175 us (14%)
  local copies, waits for them, and re-layouts  153 us (12%)
  matrix products  133 us (10%)
  loops' own time  65.5 us (5%)
  starting transfers between devices  47.6 us (4%)
  between operations  14.9 us (1%)
    all_gather x1, waiting for transfers between devices, on_device(): lax.all_gather(matmul(mixed_low, out_all).astype(jnp.bfloat16), 'tensor')  220 us
    reduce_scatter x1, waiting for transfers between devices, in_one_piece(): lax.psum_scatter(both, axis, scatter_dimension=dim, tiled=True)  118 us
    all_gather x3, waiting for transfers between devices, sent_together(): lax.all_gather(both, axis, axis=dim, tiled=True)  95.1 us
    psum x1, waiting for transfers between devices, on_device(): lax.psum(matmul(hidden_low, down_all).astype(jnp.bfloat16), 'tensor')  88.5 us
    psum x1, waiting for transfers between devices, on_device(): lax.psum(cols_inner(grad_pre_low, up_all).astype(jnp.bfloat16), 'tensor')  86.1 us
    unnamed x111, local copies, waits for them, and re-layouts  75.1 us
    unnamed x11, waiting for transfers between devices  60.3 us
    reduce_or x48, other arithmetic, advance(): jnp.any(allowed)  58 us
  transfers between devices with their start and end apart: 18, of which 15 were waited for; matrix products, arithmetic and copies ran while one was open for 19% of the time, Pallas kernels for 0%

profile of v1, /device:TPU:3, one launch (start us, length us, event | category | flops | bytes accessed | tf_op | source)
XLA Modules:
  0.0 1278.7 jit_solution(7326044562958034173)
XLA Ops:
  15.9 46.1 %all-gather.6.cloned.1.call-done = bf16[2048,1792]{1,0:T(8,128)(2,1)} async-done(((bf16[128,1792]{1,0:T(8,128)(2,1)}), bf16[2048,1792]{1,0:T(8,128)(2,1)}) %all-gather.6.cloned.1.call-update) | async-done | bytes 7340048 | tf_op jit(solution)/shard_map/all_gather | solution.py:14
  72.3 49.0 %all-gather.8.cloned.1.call-done = bf16[8192,512]{0,1:T(8,128)(2,1)} async-done(((bf16[512,512]{0,1:T(8,128)(2,1)}), bf16[8192,512]{0,1:T(8,128)(2,1)}) %all-gather.8.cloned.1.call-update) | async-done | bytes 8388624 | tf_op jit(solution)/shard_map/all_gather | solution.py:14
  130.2 7.9 copy.143
  138.1 76.3 %while.57 = (s32[]{:T(128)}, f32[2,512]{1,0:T(2,128)S(1)}, f32[2,512]{1,0:T(2,128)S(1)}, s32[16]{0:T(128)S(1)}, s32[32]{0:T(128)S(1)}, /*index=5*/s32[512]{0:T(5...) while((s32[]{:T(128)}, f32[2,512]{1,0:T(2,128)S(1)}, ...), condition=%wide.region_10.11_spmd.clone.clone, body=%wide.region_3.0_spmd.clone.clone.sunk | while | flops 140081152 | bytes 5585795 | solution.py:181
  220.3 7.9 copy.145
  228.3 76.4 %while.58 = (s32[]{:T(128)}, f32[2,512,128]{2,1,0:T(8,128)S(1)}, s32[16]{0:T(128)S(1)}, s32[32]{0:T(128)S(1)}, s32[512]{0:T(512)S(1)}, /*index=5*/bf16[16,512,2,...) while((s32[]{:T(128)}, f32[2,512,128]{2,1,0:T(8,128)S(1)}, ...), condition=%wide.region_16.17_spmd.clone.clone, body=%wide.region_11.16_spmd.clone.clone.sunk | while | flops 272330752 | bytes 2391411 | solution.py:206
  308.3 220.5 %all-gather.12.cloned.1.call-done = bf16[4096,2048]{1,0:T(8,128)(2,1)} async-done(((bf16[512,2048]{1,0:T(8,128)(2,1)}), bf16[4096,2048]{1,0:T(8,128)(2,1)}) %all-gather.12.cloned.1.call-update) | async-done | bytes 16777232 | tf_op jit(solution)/shard_map/all_gather | solution.py:210
  528.7 11.3 reduce_sum.341
  543.7 10.5 multiply_convert_fusion
  562.3 86.1 %all-reduce.4.cloned.1.call-done = bf16[512,2048]{1,0:T(8,128)(2,1)} async-done(((bf16[512,2048]{1,0:T(8,128)(2,1)}), bf16[512,2048]{1,0:T(8,128)(2,1)}) %all-reduce.4.cloned.1.call-update) | async-done | bytes 2097168 | tf_op jit(solution)/shard_map/psum | solution.py:232
  660.9 140.2 %while.59 = (s32[]{:T(128)}, f32[512,2,128]{2,0,1:T(8,128)S(1)}, bf16[16,512,2,128]{3,1,2,0:T(8,128)(2,1)}, bf16[16,512,2,128]{3,1,2,0:T(8,128)(2,1)}, s32[16]{0...) while((s32[]{:T(128)}, f32[512,2,128]{2,0,1:T(8,128)S(1)}, ...), condition=%wide.region_30.31_spmd.clone.clone, body=%wide.region_25.30_spmd.clone.clone.sunk | while | flops 676950016 | bytes 15504335 | solution.py:285
  801.1 7.8 copy.154
  808.9 8.4 copy.183
  817.3 8.0 copy.153
  825.4 8.5 copy.182
  833.8 7.7 pad_maximum_fusion
  849.6 7.8 copy.172
  857.9 6.2 fusion.121
  868.3 118.5 %reduce-scatter.8.cloned.1.call-done = bf16[512,512]{0,1:T(8,128)(2,1)} async-done(((bf16[8192,512]{0,1:T(8,128)(2,1)}), bf16[512,512]{0,1:T(8,128)(2,1)}) %reduce-scatter.8.cloned.1.call-update) | async-done | bytes 524304 | tf_op jit(solution)/shard_map/reduce_scatter | solution.py:28
  1003.5 10.1 copy.170
  1015.7 6.1 all-to-all-start.7
  1088.3 88.5 %all-reduce.6.cloned.1.call-done = (bf16[512,2048]{1,0:T(8,128)(2,1)}, bf16[512,2048]{1,0:T(8,128)(2,1)}) async-done(((bf16[512,2048]{1,0:T(8,128)(2,1)}, bf16[512,2048]{1,0:T(8,128)(2,1)}), (bf16[512,2048]{1,0:T(8,128)(2,1)}, bf16[512,2048]{1,0:T(8,128)(2,1)})) %all-reduce.6.cloned.1.call-update) | async-done | bytes 4194320 | tf_op jit(solution)/shard_map/psum | solution.py:221
  1197.6 7.2 fusion.101
  1206.1 60.2 %reduce-scatter.10.cloned.1.call-done = bf16[128,1792]{1,0:T(8,128)(2,1)} async-done(((bf16[2048,1792]{1,0:T(8,128)(2,1)}), bf16[128,1792]{1,0:T(8,128)(2,1)}) %reduce-scatter.10.cloned.1.call-update) | async-done | bytes 458768
  (728 shorter events, 495.8 us)
Async XLA Ops:
  7.2 54.8 %all-gather.6.cloned.1.call-start = ((), (), s32[]{:S(2)}) async-start(), calls=%async_computation.12 | async-start | bytes 7798784 | tf_op jit(solution)/shard_map/all_gather | solution.py:14
  12.0 109.3 %all-gather.8.cloned.1.call-start = ((), (), s32[]{:S(2)}) async-start(), calls=%async_computation.13 | async-start | bytes 8912896 | tf_op jit(solution)/shard_map/all_gather | solution.py:14
  68.2 236.7 %all-gather.10.cloned.1.call-start = ((), (), s32[]{:S(2)}) async-start(), calls=%async_computation.14 | async-start | bytes 5570560 | tf_op jit(solution)/shard_map/all_gather | solution.py:14
  69.1 459.7 %all-gather.12.cloned.1.call-start = ((), (), s32[]{:S(2)}) async-start(), calls=%async_computation.17 | async-start | bytes 18874368 | tf_op jit(solution)/shard_map/all_gather | solution.py:210
  304.7 235.4 %copy-start.7 = (bf16[512,2,128]{2,0,1:T(8,128)(2,1)}, bf16[512,2,128]{2,0,1:T(8,128)(2,1)S(1)}, u32[]{:S(2)}) copy-start(bf16[512,2,128]{2,0,1:T(8,128)(2,1)S(1)} %get-tuple-element.1875) | copy-start | bytes 786436
  304.8 235.2 %copy-start.11 = (bf16[2,512,128]{1,2,0:T(8,128)(2,1)}, bf16[2,512,128]{1,2,0:T(8,128)(2,1)S(1)}, u32[]{:S(2)}) copy-start(bf16[2,512,128]{1,2,0:T(8,128)(2,1)S(1)} %copy.146) | copy-start | bytes 786436
  308.2 340.2 %all-reduce.4.cloned.1.call-start = ((), (), s32[]{:S(2)}) async-start(), calls=%async_computation.15 | async-start | bytes 4194304 | tf_op jit(solution)/shard_map/psum | solution.py:232
  562.3 424.5 %reduce-scatter.8.cloned.1.call-start = ((), (), s32[]{:S(2)}) async-start(), calls=%async_computation.16 | async-start | bytes 8912896 | tf_op jit(solution)/shard_map/reduce_scatter | solution.py:28
  841.5 242.0 %reduce-scatter.12.cloned.1.call-start = ((), (), s32[]{:S(2)}) async-start(), calls=%async_computation.19 | async-start | bytes 5570560
  857.5 319.3 %all-reduce.6.cloned.1.call-start = ((), (), s32[]{:S(2)}) async-start(), calls=%async_computation.20 | async-start | bytes 8388608 | tf_op jit(solution)/shard_map/psum | solution.py:221
  992.8 273.6 %reduce-scatter.10.cloned.1.call-start = ((), (), s32[]{:S(2)}) async-start(), calls=%async_computation.18 | async-start | bytes 7798784
  1013.6 163.1 %copy-start.20 = (f32[2048]{0:T(1024)S(1)}, f32[2048]{0:T(1024)}, u32[]{:S(2)}) copy-start(f32[2048]{0:T(1024)} %param.32) | copy-start | bytes 24580
  1013.6 163.1 %copy-start.22 = (f32[512]{0:T(512)S(1)}, f32[512]{0:T(512)}, u32[]{:S(2)}) copy-start(f32[512]{0:T(512)} %copy-done.21) | copy-start | bytes 6148
  1013.7 163.1 %copy-start.24 = (f32[512]{0:T(512)S(1)}, f32[512]{0:T(512)}, u32[]{:S(2)}) copy-start(f32[512]{0:T(512)} %copy-done.23) | copy-start | bytes 6148
  1015.7 10.8 all-to-all-start.7
  1026.5 9.2 all-to-all-start.2
  1035.7 9.9 all-to-all-start.4
  1045.6 9.8 all-to-all-start.5
  1055.4 9.7 all-to-all-start.6
  1065.0 9.6 all-to-all-start.8
  1078.1 9.6 all-to-all-start.3
  1086.3 111.2 %copy-start.27 = (f32[2048]{0:T(1024)S(1)}, f32[2048]{0:T(1024)}, u32[]{:S(2)}) copy-start(f32[2048]{0:T(1024)} %param.46) | copy-start | bytes 24580
  1181.9 10.0 all-to-all-start
  1191.9 12.9 %all-to-all-start.1 = ((bf16[16,2,1024]{2,1,0:T(2,128)(2,1)}), bf16[16,2,1024]{2,1,0:T(2,128)(2,1)S(1)}, u32[]{:S(2)}, u32[]{:S(2)}) async-start(bf16[16,2,1024]{2,1,0:T(2,128)(2,1)} %reshape.434), calls=%async_computation.2 | async-start | bytes 131072 | tf_op jit(solution)/shard_map/all_to_all | solution.py:34
  (38 other events, 347.0 us)
Sparse Core Ops, SparseCore 0:
  12.2 49.8 all-gather.5
  68.3 52.9 all-gather.7
  123.5 49.9 all-gather.9
  308.3 220.3 all-gather.11
  562.4 85.9 all-reduce.3
  841.7 145.0 reduce-scatter.7
  989.1 68.3 reduce-scatter.11
  1060.6 116.0 all-reduce.5
  1179.1 87.1 reduce-scatter.9
